TPU v7x, 32 devices: a whole 2x2x4 slice. The times are simulated.
32 devices in a mesh: gx: 4 (over y, x), gy: 8 (over z, core).
Axes of the slice: x: 2, y: 2, z: 4, core: 2. Of those that a mesh axis runs over, the one named last changes fastest.
Arguments:
- layer_in: bfloat16 [16384, 768], P(('gx', 'gy')), may hold values from -6 to 6
- doc_ids: int32 [32, 512], P('gx'), may hold values from 0 to 7, never falling along the last dimension, each value on 1 to 128 neighbouring positions
- mix_gain: bfloat16 [768], P(('gx', 'gy')), may hold values from 0.5 to 1.5
- value_weight: bfloat16 [768, 768], P('gx', 'gy'), may hold values from -0.21875 to 0.21875
- mixing: bfloat16 [12, 512, 512], P(None, 'gy', 'gx'), may hold values from -9 to 9
- output_weight: bfloat16 [768, 768], P('gy', 'gx'), may hold values from -0.875 to 0.875
- ffn_gain: bfloat16 [768], P(('gx', 'gy')), may hold values from 0.5 to 1.5
- up_weight: bfloat16 [768, 3072], P('gx', 'gy'), may hold values from -0.21875 to 0.21875
- down_weight: bfloat16 [3072, 768], P('gy', 'gx'), may hold values from -0.109375 to 0.109375
- cotangent: bfloat16 [16384, 768], P(('gx', 'gy')), may hold values from -6 to 6
Outputs:
- layer_out: bfloat16 [16384, 768], P(('gx', 'gy'))
- grad_in: float32 [16384, 768], P(('gx', 'gy'))
- grad_mix_gain: float32 [768], P(('gx', 'gy'))
- grad_value: float32 [768, 768], P('gx', 'gy')
- grad_mixing: float32 [12, 512, 512], P(None, 'gy', 'gx')
- grad_output: float32 [768, 768], P('gy', 'gx')
- grad_ffn_gain: float32 [768], P(('gx', 'gy'))
- grad_up: float32 [768, 3072], P('gx', 'gy')
- grad_down: float32 [3072, 768], P('gy', 'gx')
Inputs may be any that keep to these rules, and one draw needn't show every extreme that they name: `doc_ids`: each row packs documents: ids never fall along the row, every id from 0 to 7 holds 1 to 128 tokens, and one document holds exactly 128.
All inputs are finite; a program needn't handle non-finite values.
Results may differ from a plain program's by a relative error of at most 0.025.
Values may be sent and summed in bfloat16 or wider, within the bound.
No kernel may reach another device: no remote copies, remote signals or barrier semaphores. Data moves between devices by JAX's collectives and lax.ppermute only.
A program may use at most 320 MiB of HBM per device.

v0:
```python
import math
import jax
import jax.numpy as jnp
from jax import lax
from jax.sharding import PartitionSpec as P

HS = 64
EPS = 1e-05
NEG = -1e30


def layer_norm(tok_rows, norm_gain):
    average = jnp.mean(tok_rows, axis=-1, keepdims=True)
    centred = tok_rows - average
    spread = jnp.mean(centred * centred, axis=-1, keepdims=True)
    return centred * lax.rsqrt(spread + EPS) * norm_gain


def gelu_tanh(up_vals):
    return jax.nn.gelu(up_vals, approximate=True)


def matmul(left, right):
    return jnp.dot(left, right, preferred_element_type=jnp.float32)


def matmul_nt(left, right):
    return lax.dot_general(
        left, right, (((1,), (1,)), ((), ())), preferred_element_type=jnp.float32
    )


def matmul_tn(left, right):
    return lax.dot_general(
        left, right, (((0,), (0,)), ((), ())), preferred_element_type=jnp.float32
    )


def masked_scores(doc_rows, heads_mix):
    same_doc = doc_rows[:, :, None] == doc_rows[:, None, :]
    return jnp.where(same_doc[:, None], heads_mix[None], NEG)


def to_groups(columns, select):
    return columns[:, None, :] * select[None]


def from_groups(grouped):
    return jnp.sum(grouped, axis=1)


def column_heads(col_width, head_total, head_size):
    col_start = lax.axis_index("gy") * col_width
    head_count = min(head_total, (col_width - 1) // head_size + 2)
    head_start = jnp.minimum(col_start // head_size, head_total - head_count)
    owner = (col_start + jnp.arange(col_width, dtype=jnp.int32)) // head_size - head_start
    select = (owner[None, :] == jnp.arange(head_count, dtype=jnp.int32)[:, None]).astype(
        jnp.bfloat16
    )
    return (head_start, head_count, select)


def mixer_forward(grouped, doc_rows, heads_mix):
    seq_count, length = doc_rows.shape
    groups, group_width = (grouped.shape[1], grouped.shape[2])
    per_block = math.gcd(seq_count, 8)
    blocks = seq_count // per_block
    vals_blocks = grouped.reshape(blocks, per_block, length, groups, group_width)
    doc_blocks = doc_rows.reshape(blocks, per_block, length)

    def block_fn(block_item):
        block_docs, block_vals = block_item
        scores = masked_scores(block_docs, heads_mix)
        row_top = jnp.max(scores, axis=-1, keepdims=True)
        expo_vals = jnp.exp(scores - row_top)
        row_total = jnp.sum(expo_vals, axis=-1, keepdims=True)
        mix_probs = (expo_vals / row_total).astype(jnp.bfloat16)
        mix_out = jnp.einsum(
            "sgqk,skgw->sqgw", mix_probs, block_vals, preferred_element_type=jnp.float32
        )
        return (mix_out, (row_top + jnp.log(row_total))[..., 0])

    mix_out, log_sums = lax.map(block_fn, (doc_blocks, vals_blocks))
    return (mix_out.reshape(seq_count * length, groups, group_width), log_sums)


def mixer_backward(grouped, grad_groups, doc_rows, log_sums, heads_mix):
    seq_count, length = doc_rows.shape
    groups, group_width = (grouped.shape[1], grouped.shape[2])
    per_block = math.gcd(seq_count, 8)
    blocks = seq_count // per_block
    vals_blocks = grouped.reshape(blocks, per_block, length, groups, group_width)
    grad_blocks = grad_groups.reshape(blocks, per_block, length, groups, group_width)
    doc_blocks = doc_rows.reshape(blocks, per_block, length)

    def block_fn(mix_acc, block_item):
        block_docs, block_vals, block_grads, block_sums = block_item
        scores = masked_scores(block_docs, heads_mix)
        mix_probs = jnp.exp(scores - block_sums[..., None])
        vals_grad = jnp.einsum(
            "sgqk,sqgw->skgw",
            mix_probs.astype(jnp.bfloat16),
            block_grads,
            preferred_element_type=jnp.float32,
        )
        probs_grad = jnp.einsum(
            "sqgw,skgw->sgqk", block_grads, block_vals, preferred_element_type=jnp.float32
        )
        score_grad = mix_probs * (
            probs_grad - jnp.sum(mix_probs * probs_grad, axis=-1, keepdims=True)
        )
        return (mix_acc + jnp.sum(score_grad, axis=0), vals_grad)

    mix_init = jnp.zeros(heads_mix.shape, jnp.float32)
    mix_grad, vals_grad = lax.scan(
        block_fn, mix_init, (doc_blocks, vals_blocks, grad_blocks, log_sums)
    )
    return (vals_grad.reshape(seq_count * length, groups, group_width), mix_grad)


def shards(
    layer_in,
    doc_ids,
    mix_gain,
    value_weight,
    mixing,
    output_weight,
    ffn_gain,
    up_weight,
    down_weight,
    cotangent,
):
    mixing_part, gain_one_part, gain_two_part = (
        lax.all_gather(mixing, "gy", axis=1, tiled=True),
        lax.all_gather(mix_gain, "gy", axis=0, tiled=True),
        lax.all_gather(ffn_gain, "gy", axis=0, tiled=True),
    )
    value_cols, up_cols, output_rows, down_rows, mix_full, gain_one, gain_two = (
        lax.all_gather(value_weight, "gx", axis=0, tiled=True),
        lax.all_gather(up_weight, "gx", axis=0, tiled=True),
        lax.all_gather(output_weight, "gx", axis=1, tiled=True),
        lax.all_gather(down_weight, "gx", axis=1, tiled=True),
        lax.all_gather(mixing_part, "gx", axis=2, tiled=True),
        lax.all_gather(gain_one_part, "gx", axis=0, tiled=True),
        lax.all_gather(gain_two_part, "gx", axis=0, tiled=True),
    )
    gain_one = gain_one.astype(jnp.float32)
    gain_two = gain_two.astype(jnp.float32)
    layer_vals = layer_in.astype(jnp.float32)
    cot_vals = cotangent.astype(jnp.float32)
    normed_low = layer_norm(layer_vals, gain_one).astype(jnp.bfloat16)
    normed_all = lax.all_gather(normed_low, "gy", axis=0, tiled=True)
    head_start, head_count, select = column_heads(value_cols.shape[1], mix_full.shape[0], HS)
    heads_mix = lax.dynamic_slice_in_dim(mix_full, head_start, head_count, 0).astype(jnp.float32)
    value_low = matmul(normed_all, value_cols).astype(jnp.bfloat16)
    grouped = to_groups(value_low, select)
    mix_out, log_sums = mixer_forward(grouped, doc_ids, heads_mix)
    mixed_low = from_groups(mix_out).astype(jnp.bfloat16)
    middle = layer_vals + lax.psum_scatter(
        matmul(mixed_low, output_rows), "gy", scatter_dimension=0, tiled=True
    )
    normed_two = layer_norm(middle, gain_two).astype(jnp.bfloat16)
    normed_two_all = lax.all_gather(normed_two, "gy", axis=0, tiled=True)
    up_vals = matmul(normed_two_all, up_cols)
    act_low = gelu_tanh(up_vals).astype(jnp.bfloat16)
    layer_out = (
        middle
        + lax.psum_scatter(
            matmul(act_low, down_rows).astype(jnp.bfloat16), "gy", scatter_dimension=0, tiled=True
        ).astype(jnp.float32)
    ).astype(jnp.bfloat16)
    cot_all = lax.all_gather(cotangent, "gy", axis=0, tiled=True)
    down_grad = matmul_tn(act_low, cot_all)
    act_grad = matmul_nt(cot_all, down_rows)
    gelu_out, gelu_back = jax.vjp(gelu_tanh, up_vals)
    up_grad_low = gelu_back(act_grad)[0].astype(jnp.bfloat16)
    up_weight_grad = matmul_tn(normed_two_all, up_grad_low)
    normed_two_grad = lax.psum_scatter(
        matmul_nt(up_grad_low, up_cols).astype(jnp.bfloat16), "gy", scatter_dimension=0, tiled=True
    ).astype(jnp.float32)
    norm_out, norm_back = jax.vjp(layer_norm, middle, gain_two)
    mid_norm_grad, gain_two_grad = norm_back(normed_two_grad)
    mid_grad = cot_vals + mid_norm_grad
    branch_low = mid_grad.astype(jnp.bfloat16)
    branch_all = lax.all_gather(branch_low, "gy", axis=0, tiled=True)
    output_grad = matmul_tn(mixed_low, branch_all)
    mixed_grad_low = matmul_nt(branch_all, output_rows).astype(jnp.bfloat16)
    vals_grad, mix_grad_local = mixer_backward(
        grouped, to_groups(mixed_grad_low, select), doc_ids, log_sums, heads_mix
    )
    value_grad_low = from_groups(vals_grad).astype(jnp.bfloat16)
    value_grad = matmul_tn(normed_all, value_grad_low)
    normed_one_grad = lax.psum_scatter(
        matmul_nt(value_grad_low, value_cols).astype(jnp.bfloat16),
        "gy",
        scatter_dimension=0,
        tiled=True,
    ).astype(jnp.float32)
    mix_grad_full = lax.dynamic_update_slice_in_dim(
        jnp.zeros(mix_full.shape, jnp.float32), mix_grad_local, head_start, 0
    )
    first_out, first_back = jax.vjp(layer_norm, layer_vals, gain_one)
    in_norm_grad, gain_one_grad = first_back(normed_one_grad)
    grad_in = mid_grad + in_norm_grad
    (
        value_grad,
        up_weight_grad,
        output_grad,
        down_grad,
        mix_grad_part,
        gain_one_part_grad,
        gain_two_part_grad,
    ) = (
        lax.psum_scatter(
            value_grad.astype(jnp.bfloat16), "gx", scatter_dimension=0, tiled=True
        ).astype(jnp.float32),
        lax.psum_scatter(
            up_weight_grad.astype(jnp.bfloat16), "gx", scatter_dimension=0, tiled=True
        ).astype(jnp.float32),
        lax.psum_scatter(
            output_grad.astype(jnp.bfloat16), "gx", scatter_dimension=1, tiled=True
        ).astype(jnp.float32),
        lax.psum_scatter(
            down_grad.astype(jnp.bfloat16), "gx", scatter_dimension=1, tiled=True
        ).astype(jnp.float32),
        lax.psum_scatter(
            mix_grad_full.astype(jnp.bfloat16), "gx", scatter_dimension=2, tiled=True
        ).astype(jnp.float32),
        lax.psum_scatter(
            gain_one_grad.astype(jnp.bfloat16), "gx", scatter_dimension=0, tiled=True
        ).astype(jnp.float32),
        lax.psum_scatter(
            gain_two_grad.astype(jnp.bfloat16), "gx", scatter_dimension=0, tiled=True
        ).astype(jnp.float32),
    )
    mix_grad_out, gain_one_out, gain_two_out = (
        lax.psum_scatter(
            mix_grad_part.astype(jnp.bfloat16), "gy", scatter_dimension=1, tiled=True
        ).astype(jnp.float32),
        lax.psum_scatter(
            gain_one_part_grad.astype(jnp.bfloat16), "gy", scatter_dimension=0, tiled=True
        ).astype(jnp.float32),
        lax.psum_scatter(
            gain_two_part_grad.astype(jnp.bfloat16), "gy", scatter_dimension=0, tiled=True
        ).astype(jnp.float32),
    )
    return (
        layer_out,
        grad_in,
        gain_one_out,
        value_grad,
        mix_grad_out,
        output_grad,
        gain_two_out,
        up_weight_grad,
        down_grad,
    )


def solution(mesh):
    in_specs = (
        P(("gx", "gy"), None),
        P("gx", None),
        P(("gx", "gy")),
        P("gx", "gy"),
        P(None, "gy", "gx"),
        P("gy", "gx"),
        P(("gx", "gy")),
        P("gx", "gy"),
        P("gy", "gx"),
        P(("gx", "gy"), None),
    )
    out_specs = (
        P(("gx", "gy"), None),
        P(("gx", "gy"), None),
        P(("gx", "gy")),
        P("gx", "gy"),
        P(None, "gy", "gx"),
        P("gy", "gx"),
        P(("gx", "gy")),
        P("gx", "gy"),
        P("gy", "gx"),
    )
    return jax.shard_map(shards, mesh=mesh, in_specs=in_specs, out_specs=out_specs, check_vma=False)
```

profile of v0, /device:TPU:0, one launch (start us, length us, event | category | flops | bytes accessed | tf_op | source)
XLA Modules:
  0.0 1063.9 jit_solution(16108159190764218038)
XLA Ops:
  12.4 18.4 %all-reduce.9 = (bf16[192]{0:T(256)(128)(2,1)S(1)}, bf16[192]{0:T(256)(128)(2,1)S(1)}) all-reduce(bf16[192]{0:T(256)(128)(2,1)S(1)} %dynamic-update-slice, bf16[192]{0:T(256)(128)(2,1)S(1)} %dynamic-update-slice.2), channel_id=1, replica_groups=mesh['gx'=4,'gy'=8] {'gy'}, use_global_device_ids=true, to_apply=%add | all-reduce | flops 384 | bytes 1536
  31.2 9.9 all-reduce.11
  47.3 8.2 all_gather.48
  55.5 8.3 all_gather.47
  65.2 42.3 %all-gather.11.cloned.1.call-done = bf16[4096,768]{1,0:T(8,128)(2,1)} async-done(((bf16[512,768]{1,0:T(8,128)(2,1)}), bf16[4096,768]{1,0:T(8,128)(2,1)}) %all-gather.11.cloned.1.call-update) | async-done | bytes 6291472 | tf_op jit(solution)/shard_map/all_gather | solution.py:152
  107.5 4.8 convolution_convert_fusion.4
  113.4 64.7 %all-gather.9.cloned.1.call-done = bf16[12,512,512]{2,1,0:T(8,128)(2,1)} async-done(((bf16[12,512,128]{2,1,0:T(8,128)(2,1)}), bf16[12,512,512]{2,1,0:T(8,128)(2,1)}) %all-gather.9.cloned.1.call-update) | async-done | bytes 6291472 | tf_op jit(solution)/shard_map/all_gather | solution.py:143
  178.1 3.6 dynamic-slice_convert_fusion
  181.6 4.0 copy.31
  185.6 4.3 select_reduce_fusion
  190.0 4.8 fusion.3
  194.8 7.5 fusion.72
  202.4 6.4 fusion.103
  209.5 128.7 %reduce-scatter.15.cloned.1.call-done = f32[512,768]{1,0:T(8,128)} async-done(((f32[4096,768]{1,0:T(8,128)}), f32[512,768]{1,0:T(8,128)}) %reduce-scatter.15.cloned.1.call-update) | async-done | bytes 1572880 | tf_op jit(solution)/shard_map/reduce_scatter | solution.py:159
  341.4 11.7 %all_gather.52 = bf16[768,384]{1,0:T(8,128)(2,1)} all-gather(bf16[192,384]{1,0:T(8,128)(2,1)S(1)} %copy-done.14), channel_id=1, replica_groups=mesh['gx'=4,'gy'=8] {'gx'}, dimensions={0}, use_global_device_ids=true | all-gather | bytes 737280 | tf_op jit(solution)/shard_map/all_gather | solution.py:140
  353.2 10.3 all_gather.53
  363.5 39.3 %all-gather.15.cloned.1.call-done = bf16[4096,768]{1,0:T(8,128)(2,1)} async-done(((bf16[512,768]{1,0:T(8,128)(2,1)}), bf16[4096,768]{1,0:T(8,128)(2,1)}) %all-gather.15.cloned.1.call-update) | async-done | bytes 6291472 | tf_op jit(solution)/shard_map/all_gather | solution.py:172
  402.8 8.9 fusion.104
  411.7 56.6 %all-gather.13.cloned.1.call-done = bf16[4096,768]{1,0:T(8,128)(2,1)} async-done(((bf16[512,768]{1,0:T(8,128)(2,1)}), bf16[4096,768]{1,0:T(8,128)(2,1)}) %all-gather.13.cloned.1.call-update) | async-done | bytes 6291472 | tf_op jit(solution)/shard_map/all_gather | solution.py:163
  468.4 13.7 %fusion.31 = (bf16[4096,384]{1,0:T(8,128)(2,1)S(1)}, f32[4096,384]{1,0:T(8,128)}) fusion(f32[4096,384]{1,0:T(8,128)} %fusion.104, bf16[4096,768]{1,0:T(8,128)(2,1)} %all-gather.13.cloned.1.call-done, bf16[768,384]{1,0:T(8,128)(2,1)} %all_gather.52), kind=kOutput, calls=%fused_computation.36 | convolution fusion | flops 2447376384 | bytes 22609920 | tf_op jit(solution)/shard_map/dot_general | solution.py:24
  483.7 5.4 convolution_convert_fusion.1
  489.1 9.9 convolution_convert_fusion.2
  499.1 58.6 %reduce-scatter.19.cloned.1.call-done = bf16[512,768]{1,0:T(8,128)(2,1)} async-done(((bf16[4096,768]{1,0:T(8,128)(2,1)}), bf16[512,768]{1,0:T(8,128)(2,1)}) %reduce-scatter.19.cloned.1.call-update) | async-done | bytes 786448 | tf_op jit(solution)/shard_map/reduce_scatter | solution.py:178
  559.5 68.6 %reduce-scatter.17.cloned.1.call-done = bf16[512,768]{1,0:T(8,128)(2,1)} async-done(((bf16[4096,768]{1,0:T(8,128)(2,1)}), bf16[512,768]{1,0:T(8,128)(2,1)}) %reduce-scatter.17.cloned.1.call-update) | async-done | bytes 786448 | tf_op jit(solution)/shard_map/reduce_scatter | solution.py:168
  628.2 2.9 fusion.99
  634.0 62.8 %all-gather.17.cloned.1.call-done = bf16[4096,768]{1,0:T(8,128)(2,1)} async-done(((bf16[512,768]{1,0:T(8,128)(2,1)}), bf16[4096,768]{1,0:T(8,128)(2,1)}) %all-gather.17.cloned.1.call-update) | async-done | bytes 6291472 | tf_op jit(solution)/shard_map/all_gather | solution.py:185
  696.7 4.8 convolution_convert_fusion.3
  702.6 16.4 %fusion = f32[8,3,512,512]{2,3,1,0:T(8,128)} fusion(f32[8,3,512]{2,1,0:T(4,128)S(1)} %log_add_fusion, f32[3,512,512]{1,2,0:T(8,128)} %copy.31, pred[8,512,512]{1,2,0:T(8,128)(4,1)S(1)} %copy-done.5, bf16[8,512,96]{1,2,0:T(8,128)(2,1)} %bitcast.68, bf16[3,96]{1,0:T(4,128)(2,1)S(1)} %fusion.92, bf16[8,512,96]{1,2,0:T(8,128)(2,1)} %bitcast.65), kind=kOutput, calls=%fused_computation | convolution fusion | flops 1229206016 | bytes 32031296 | tf_op jit(solution)/shard_map/while/body/eval_jaxpr/sub | solution.py:110
  719.0 15.5 %fusion.9 = bf16[3,512,512]{1,2,0:T(8,128)(2,1)} fusion(f32[8,3,512,512]{2,3,1,0:T(8,128)} %fusion, f32[8,3,512]{2,1,0:T(4,128)S(1)} %log_add_fusion, f32[3,512,512]{1,2,0:T(8,128)} %copy.31, pred[8,512,512]{1,2,0:T(8,128)(4,1)S(1)} %copy-done.5, bf16[3,96]{1,0:T(4,128)(2,1)S(1)} %fusion.92, bf16[8,512,96]{1,2,0:T(8,128)(2,1)} %bitcast.66, ...), kind=kOutput, calls=%fused_computation.12 | convolution fusion | flops 1240989696 | bytes 33604160 | tf_op jit(solution)/shard_map/while/body/eval_jaxpr/sqgw,skgw->sgqk/dot_general | solution.py:106
  737.1 3.2 broadcast_in_dim.115
  741.6 14.6 %copy.44 = bf16[12,512,512]{1,0,2:T(8,128)(2,1)} copy(bf16[12,512,512]{2,1,0:T(8,128)(2,1)} %constant_dynamic-update-slice_fusion) | data formatting | bytes 12582912
  756.2 13.4 %copy.52 = bf16[64,8,12,512]{3,1,2,0:T(8,128)(2,1)} copy(bf16[64,8,12,512]{3,2,1,0:T(8,128)(2,1)} %bitcast.56) | data formatting | bytes 12582912
  769.7 8.9 convolution_convert_fusion.5
  778.9 8.0 convolution_convert_fusion.6
  787.0 4.3 convolution_convert_fusion.8
  792.2 9.2 fusion.67
  802.7 5.5 convolution_convert_fusion.7
  808.5 4.5 convolution_convert_fusion
  813.0 25.6 %reduce-scatter.31.cloned.1.call-done = bf16[128,6144]{1,0:T(8,128)(2,1)} async-done(((bf16[512,6144]{1,0:T(8,128)(2,1)}), bf16[128,6144]{1,0:T(8,128)(2,1)}) %reduce-scatter.31.cloned.1.call-update) | async-done | bytes 1572880
  845.8 20.7 %reduce-scatter.29.cloned.1.call-done = bf16[384,192]{0,1:T(8,128)(2,1)} async-done(((bf16[384,768]{0,1:T(8,128)(2,1)}), bf16[384,192]{0,1:T(8,128)(2,1)}) %reduce-scatter.29.cloned.1.call-update) | async-done | bytes 147472 | tf_op jit(solution)/shard_map/reduce_scatter | solution.py:223
  868.2 26.4 %reduce-scatter.27.cloned.1.call-done = bf16[192,384]{1,0:T(8,128)(2,1)} async-done(((bf16[768,384]{1,0:T(8,128)(2,1)}), bf16[192,384]{1,0:T(8,128)(2,1)}) %reduce-scatter.27.cloned.1.call-update) | async-done | bytes 147472 | tf_op jit(solution)/shard_map/reduce_scatter | solution.py:217
  896.3 25.1 %reduce-scatter.33.cloned.1.call-done = bf16[192,96]{1,0:T(8,128)(2,1)} async-done(((bf16[768,96]{1,0:T(8,128)(2,1)}), bf16[192,96]{1,0:T(8,128)(2,1)}) %reduce-scatter.33.cloned.1.call-update) | async-done | bytes 36880
  923.0 25.7 %reduce-scatter.23.cloned.1.call-done = bf16[192,96]{1,0:T(8,128)(2,1)} async-done(((bf16[768,96]{1,0:T(8,128)(2,1)}), bf16[192,96]{1,0:T(8,128)(2,1)}) %reduce-scatter.23.cloned.1.call-update) | async-done | bytes 36880 | tf_op jit(solution)/shard_map/reduce_scatter | solution.py:214
  950.1 70.5 %reduce-scatter.21.cloned.1.call-done = bf16[512,768]{1,0:T(8,128)(2,1)} async-done(((bf16[4096,768]{1,0:T(8,128)(2,1)}), bf16[512,768]{1,0:T(8,128)(2,1)}) %reduce-scatter.21.cloned.1.call-update) | async-done | bytes 786448 | tf_op jit(solution)/shard_map/reduce_scatter | solution.py:193
  1024.4 9.8 all-reduce.10
  1034.4 13.7 %all-reduce.8 = (bf16[192]{0:T(256)(128)(2,1)S(1)}, bf16[192]{0:T(256)(128)(2,1)S(1)}) all-reduce(bf16[192]{0:T(256)(128)(2,1)S(1)} %dynamic-slice.6, bf16[192]{0:T(256)(128)(2,1)S(1)} %dynamic-slice.10), channel_id=7, replica_groups=mesh['gx'=4,'gy'=8] {'gy'}, use_global_device_ids=true, to_apply=%region_16.17.clone | all-reduce | flops 384 | bytes 1536
  1049.3 3.0 add_add_fusion.2
  1052.3 3.2 reduce-scatter.25.cloned.1.call-done
  (142 shorter events, 49.8 us)
Async XLA Ops:
  7.2 40.0 %copy-start.21 = (bf16[96,192]{1,0:T(8,128)(2,1)S(1)}, bf16[96,192]{1,0:T(8,128)(2,1)}, u32[]{:S(2)}) copy-start(bf16[96,192]{1,0:T(8,128)(2,1)} %param.15) | copy-start | bytes 110596
  7.2 48.3 %copy-start.22 = (bf16[192,96]{1,0:T(8,128)(2,1)S(1)}, bf16[192,96]{1,0:T(8,128)(2,1)}, u32[]{:S(2)}) copy-start(bf16[192,96]{1,0:T(8,128)(2,1)} %param.13) | copy-start | bytes 110596
  7.2 39.2 %all-gather.7.cloned.1.call-start = ((), (), s32[]{:S(2)}) async-start(), calls=%async_computation.10 | async-start | bytes 1769472 | tf_op jit(solution)/shard_map/all_gather | solution.py:134
  7.9 55.8 %copy-start.20 = (s32[8,512]{1,0:T(8,128)S(1)}, s32[8,512]{1,0:T(8,128)}, u32[]{:S(2)}) copy-start(s32[8,512]{1,0:T(8,128)} %param.11) | copy-start | bytes 49156
  7.9 99.6 %all-gather.11.cloned.1.call-start = ((), (), s32[]{:S(2)}) async-start(), calls=%async_computation.12 | async-start | bytes 7077888 | tf_op jit(solution)/shard_map/all_gather | solution.py:152
  41.1 6.0 copy-start.16
  42.4 4.7 copy-start.18
  43.9 3.2 copy-start.25
  43.9 3.2 copy-start.23
  46.3 131.8 %all-gather.9.cloned.1.call-start = ((), (), s32[]{:S(2)}) async-start(), calls=%async_computation.11 | async-start | bytes 7864320 | tf_op jit(solution)/shard_map/all_gather | solution.py:143
  47.0 291.2 %reduce-scatter.15.cloned.1.call-start = ((), (), s32[]{:S(2)}) async-start(), calls=%async_computation.13 | async-start | bytes 14155776 | tf_op jit(solution)/shard_map/reduce_scatter | solution.py:159
  63.7 48.6 %copy-start.10 = (bf16[768,96]{1,0:T(8,128)(2,1)}, bf16[768,96]{1,0:T(8,128)(2,1)S(1)}, u32[]{:S(2)}) copy-start(bf16[768,96]{1,0:T(8,128)(2,1)S(1)} %all_gather.47) | copy-start | bytes 442372
  65.2 129.5 %copy-start.4 = (pred[8,512,512]{1,2,0:T(8,128)(4,1)}, pred[8,512,512]{1,2,0:T(8,128)(4,1)S(1)}, u32[]{:S(2)}) copy-start(pred[8,512,512]{1,2,0:T(8,128)(4,1)S(1)} %broadcast_compare_fusion) | copy-start | bytes 6291460
  185.6 4.3 copy-start.3
  190.0 4.8 copy-start.12
  202.4 6.4 copy-start.6
  208.8 129.4 %copy-start = (bf16[512,768]{1,0:T(8,128)(2,1)S(1)}, bf16[512,768]{1,0:T(8,128)(2,1)}, u32[]{:S(2)}) copy-start(bf16[512,768]{1,0:T(8,128)(2,1)} %param.10) | copy-start | bytes 2359300
  208.8 194.0 %all-gather.15.cloned.1.call-start = ((), (), s32[]{:S(2)}) async-start(), calls=%async_computation.16 | async-start | bytes 7077888 | tf_op jit(solution)/shard_map/all_gather | solution.py:172
  209.4 258.9 %all-gather.13.cloned.1.call-start = ((), (), s32[]{:S(2)}) async-start(), calls=%async_computation.14 | async-start | bytes 7077888 | tf_op jit(solution)/shard_map/all_gather | solution.py:163
  339.8 1.6 copy-start.14
  339.9 13.3 %copy-start.15 = (bf16[384,192]{0,1:T(8,128)(2,1)S(1)}, bf16[384,192]{0,1:T(8,128)(2,1)}, u32[]{:S(2)}) copy-start(bf16[384,192]{0,1:T(8,128)(2,1)} %param.18) | copy-start | bytes 442372
  341.4 216.3 %reduce-scatter.19.cloned.1.call-start = ((), (), s32[]{:S(2)}) async-start(), calls=%async_computation.17 | async-start | bytes 7077888 | tf_op jit(solution)/shard_map/reduce_scatter | solution.py:178
  468.4 15.3 %copy-start.13 = (bf16[768,384]{1,0:T(8,128)(2,1)S(1)}, bf16[768,384]{1,0:T(8,128)(2,1)}, u32[]{:S(2)}) copy-start(bf16[768,384]{1,0:T(8,128)(2,1)} %all_gather.52) | copy-start | bytes 1769476
  482.0 1.6 copy-start.27
  489.1 139.1 %reduce-scatter.17.cloned.1.call-start = ((), (), s32[]{:S(2)}) async-start(), calls=%async_computation.15 | async-start | bytes 7077888 | tf_op jit(solution)/shard_map/reduce_scatter | solution.py:168
  499.0 197.7 %all-gather.17.cloned.1.call-start = ((), (), s32[]{:S(2)}) async-start(), calls=%async_computation.18 | async-start | bytes 7077888 | tf_op jit(solution)/shard_map/all_gather | solution.py:185
  559.5 72.8 %copy-start.8 = (bf16[512,768]{1,0:T(8,128)(2,1)S(1)}, bf16[512,768]{1,0:T(8,128)(2,1)}, u32[]{:S(2)}) copy-start(bf16[512,768]{1,0:T(8,128)(2,1)} %param.19) | copy-start | bytes 2359300
  631.1 1.1 copy-start.1
  633.5 205.2 %reduce-scatter.31.cloned.1.call-start = ((), (), s32[]{:S(2)}) async-start(), calls=%async_computation.24 | async-start | bytes 7864320
  633.9 68.6 %copy-start.5 = (pred[8,512,512]{1,2,0:T(8,128)(4,1)S(1)}, pred[8,512,512]{1,2,0:T(8,128)(4,1)}, u32[]{:S(2)}) copy-start(pred[8,512,512]{1,2,0:T(8,128)(4,1)} %copy-done.4) | copy-start | bytes 6291460
  737.1 3.2 copy-start.9
  769.7 96.9 %reduce-scatter.29.cloned.1.call-start = ((), (), s32[]{:S(2)}) async-start(), calls=%async_computation.23 | async-start | bytes 737280 | tf_op jit(solution)/shard_map/reduce_scatter | solution.py:223
  778.7 116.0 %reduce-scatter.27.cloned.1.call-start = ((), (), s32[]{:S(2)}) async-start(), calls=%async_computation.22 | async-start | bytes 737280 | tf_op jit(solution)/shard_map/reduce_scatter | solution.py:217
  786.9 134.5 %reduce-scatter.33.cloned.1.call-start = ((), (), s32[]{:S(2)}) async-start(), calls=%async_computation.25 | async-start | bytes 245760
  802.6 146.0 %reduce-scatter.23.cloned.1.call-start = ((), (), s32[]{:S(2)}) async-start(), calls=%async_computation.20 | async-start | bytes 245760 | tf_op jit(solution)/shard_map/reduce_scatter | solution.py:214
  802.6 5.8 copy-start.11
  808.2 212.4 %reduce-scatter.21.cloned.1.call-start = ((), (), s32[]{:S(2)}) async-start(), calls=%async_computation.19 | async-start | bytes 7077888 | tf_op jit(solution)/shard_map/reduce_scatter | solution.py:193
  813.0 242.5 %reduce-scatter.25.cloned.1.call-start = ((), (), s32[]{:S(2)}) async-start(), calls=%async_computation.21 | async-start | bytes 1769472 | tf_op jit(solution)/shard_map/reduce_scatter | solution.py:237
  841.5 179.1 %copy-start.17 = (f32[768]{0:T(1024)S(1)}, f32[768]{0:T(1024)}, u32[]{:S(2)}) copy-start(f32[768]{0:T(1024)} %copy-done.16) | copy-start | bytes 9220
  841.5 179.1 %copy-start.19 = (f32[512]{0:T(512)S(1)}, f32[512]{0:T(512)}, u32[]{:S(2)}) copy-start(f32[512]{0:T(512)} %copy-done.18) | copy-start | bytes 6148
  841.5 180.8 %copy-start.26 = (f32[512]{0:T(512)S(1)}, f32[512]{0:T(512)}, u32[]{:S(2)}) copy-start(f32[512]{0:T(512)} %copy-done.25) | copy-start | bytes 6148
  844.4 177.9 %copy-start.24 = (f32[512]{0:T(512)S(1)}, f32[512]{0:T(512)}, u32[]{:S(2)}) copy-start(f32[512]{0:T(512)} %copy-done.23) | copy-start | bytes 6148
  844.4 204.9 %copy-start.2 = (f32[512,768]{1,0:T(8,128)S(1)}, f32[512,768]{1,0:T(8,128)}, u32[]{:S(2)}) copy-start(f32[512,768]{1,0:T(8,128)} %copy-done.1) | copy-start | bytes 4718596
  1020.6 28.7 %copy-start.7 = (bf16[512,768]{1,0:T(8,128)(2,1)S(1)}, bf16[512,768]{1,0:T(8,128)(2,1)}, u32[]{:S(2)}) copy-start(bf16[512,768]{1,0:T(8,128)(2,1)} %reduce-scatter.21.cloned.1.call-done) | copy-start | bytes 2359300
Sparse Core Ops, SparseCore 0:
  9.6 27.8 all-gather.6
  46.4 61.0 all-gather.10
  109.4 68.6 all-gather.8
  208.9 129.2 reduce-scatter.14
  339.7 63.0 all-gather.14
  404.9 63.3 all-gather.12
  489.2 68.4 reduce-scatter.18
  560.0 68.1 reduce-scatter.16
  633.6 63.1 all-gather.16
  769.8 68.8 reduce-scatter.30
  841.5 25.0 reduce-scatter.28
  869.6 25.0 reduce-scatter.26
  897.4 23.9 reduce-scatter.32
  924.6 23.9 reduce-scatter.22
  950.8 69.7 reduce-scatter.20
  1022.8 32.6 reduce-scatter.24
where the time goes:
time: 1070 us; the launch traced here: 1060 us
  waiting for transfers between devices  721 us (67%)
  matrix products  134 us (13%)
  blocking collectives  90.4 us (8%)
  local copies, waits for them, and re-layouts  56.6 us (5%)
  other arithmetic  43.4 us (4%)
  between operations  17.4 us (2%)
    reduce_scatter x1, waiting for transfers between devices, shards(): lax.psum_scatter(matmul(mixed_low, output_rows), 'gy', scatter_dimension=...  129 us
    reduce_scatter x1, waiting for transfers between devices, shards(): lax.psum_scatter(matmul_nt(value_grad_low, value_cols).astype(jnp.bfloat1...  70.5 us
    reduce_scatter x1, waiting for transfers between devices, shards(): lax.psum_scatter(matmul(act_low, down_rows).astype(jnp.bfloat16), 'gy', s...  68.6 us
    all_gather x1, waiting for transfers between devices, shards(): lax.all_gather(mixing_part, 'gx', axis=2, tiled=True)  64.7 us
    all_gather x1, waiting for transfers between devices, shards(): branch_all = lax.all_gather(branch_low, 'gy', axis=0, tiled=True)  62.8 us
    reduce_scatter x1, waiting for transfers between devices, shards(): lax.psum_scatter(matmul_nt(up_grad_low, up_cols).astype(jnp.bfloat16), 'g...  58.6 us
    all_gather x1, waiting for transfers between devices, shards(): normed_two_all = lax.all_gather(normed_two, 'gy', axis=0, tiled=True)  56.6 us
    unnamed x18, waiting for transfers between devices  52.8 us
  transfers between devices with their start and end apart: 16, of which 15 were waited for; matrix products, arithmetic and copies ran while one was open for 10% of the time, Pallas kernels for 0%

commit v1 on v0

--- a/solution.py
+++ b/solution.py
@@ -1,3 +1,4 @@
+import functools
 import math
 import jax
 import jax.numpy as jnp
@@ -7,6 +8,27 @@
 HS = 64
 EPS = 1e-05
 NEG = -1e30
+
+
+def _raise_groups(local, device_axis, at_axis):
+    fan = lax.axis_size(device_axis)
+    views = tuple(((dev_i, (dev_i + 1) % fan) for dev_i in range(fan)))
+
+    def mix_strips_all(outcome_arr):
+        if len(outcome_arr) == fan:
+            return outcome_arr
+        mid_arr = mix_strips_all([lax.ppermute(outcome_arr[0], device_axis, views), *outcome_arr])
+        return mid_arr
+
+    near = mix_strips_all([local])
+    after = jnp.concatenate(near, axis=at_axis)
+    w_next = jnp.roll(
+        after, shift=(lax.axis_index(device_axis) + 1) * local.shape[at_axis], axis=at_axis
+    )
+    return w_next
+
+
+_supply_all_outputs = functools.partial(_raise_groups, device_axis="gy", at_axis=0)
 
 
 def layer_norm(tok_rows, norm_gain):
@@ -160,7 +182,7 @@
         matmul(mixed_low, output_rows), "gy", scatter_dimension=0, tiled=True
     )
     normed_two = layer_norm(middle, gain_two).astype(jnp.bfloat16)
-    normed_two_all = lax.all_gather(normed_two, "gy", axis=0, tiled=True)
+    normed_two_all = _supply_all_outputs(normed_two)
     up_vals = matmul(normed_two_all, up_cols)
     act_low = gelu_tanh(up_vals).astype(jnp.bfloat16)
     layer_out = (

time: 1070 us -> 1110 us (1.037)
  waiting for transfers between devices: 721 us -> 739 us
  local copies, waits for them, and re-layouts: 56.6 us -> 69.6 us
    ppermute x0 -> x7, waiting for transfers between devices: none -> 119 us  [mix_strips_all(): lax.ppermute(outcome_arr[0], device_axis, views)]
    all_gather x1 -> x0, waiting for transfers between devices: 56.6 us -> none  [shards(): normed_two_all = lax.all_gather(normed_two, 'gy', axis=0, tiled=True)]
    all_gather x1, waiting for transfers between devices: 39.3 us -> 0.01 us  [shards(): cot_all = lax.all_gather(cotangent, 'gy', axis=0, tiled=True)]
    unnamed x74 -> x100, local copies, waits for them, and re-layouts: 42 us -> 55.4 us
    dot_general x1, matrix products: 7.5 us -> 19.2 us  [block_fn(): jnp.einsum('sgqk,skgw->sqgw', mix_probs, block_vals, preferred_element_ty...]
    unnamed x18 -> x17, waiting for transfers between devices: 52.8 us -> 52.6 us
  transfers between devices with their start and end apart: 16 -> 22, of which waited for: 15 -> 19; matrix products, arithmetic and copies ran while one was open for 10% -> 9% of each run, Pallas kernels for 0% -> 0%
where the time goes in v1:
time: 1110 us; the launch traced here: 1100 us
  waiting for transfers between devices  739 us (67%)
  matrix products  137 us (12%)
  blocking collectives  91.5 us (8%)
  local copies, waits for them, and re-layouts  69.6 us (6%)
  other arithmetic  44.9 us (4%)
  between operations  17.5 us (2%)
    reduce_scatter x1, waiting for transfers between devices, shards(): lax.psum_scatter(matmul(mixed_low, output_rows), 'gy', scatter_dimension=...  129 us
    ppermute x7, waiting for transfers between devices, mix_strips_all(): lax.ppermute(outcome_arr[0], device_axis, views)  119 us
    reduce_scatter x1, waiting for transfers between devices, shards(): lax.psum_scatter(matmul_nt(value_grad_low, value_cols).astype(jnp.bfloat1...  70.5 us
    reduce_scatter x1, waiting for transfers between devices, shards(): lax.psum_scatter(matmul(act_low, down_rows).astype(jnp.bfloat16), 'gy', s...  68.7 us
    all_gather x1, waiting for transfers between devices, shards(): lax.all_gather(mixing_part, 'gx', axis=2, tiled=True)  64.7 us
    all_gather x1, waiting for transfers between devices, shards(): branch_all = lax.all_gather(branch_low, 'gy', axis=0, tiled=True)  63.2 us
    reduce_scatter x1, waiting for transfers between devices, shards(): lax.psum_scatter(matmul_nt(up_grad_low, up_cols).astype(jnp.bfloat16), 'g...  55.9 us
    unnamed x100, local copies, waits for them, and re-layouts  55.4 us
  transfers between devices with their start and end apart: 22, of which 19 were waited for; matrix products, arithmetic and copies ran while one was open for 9% of the time, Pallas kernels for 0%

profile of v1, /device:TPU:0, one launch (start us, length us, event | category | flops | bytes accessed | tf_op | source)
XLA Modules:
  0.0 1101.0 jit_solution(6515213711016294847)
XLA Ops:
  12.3 18.4 %all-reduce.9 = (bf16[192]{0:T(256)(128)(2,1)S(1)}, bf16[192]{0:T(256)(128)(2,1)S(1)}) all-reduce(bf16[192]{0:T(256)(128)(2,1)S(1)} %dynamic-update-slice, bf16[192]{0:T(256)(128)(2,1)S(1)} %dynamic-update-slice.2), channel_id=1, replica_groups=mesh['gx'=4,'gy'=8] {'gy'}, use_global_device_ids=true, to_apply=%add | all-reduce | flops 384 | bytes 1536
  31.2 9.9 all-reduce.11
  48.0 8.4 all_gather.44
  56.4 8.3 all_gather.45
  66.2 41.3 %all-gather.10.cloned.1.call-done = bf16[4096,768]{1,0:T(8,128)(2,1)} async-done(((bf16[512,768]{1,0:T(8,128)(2,1)}), bf16[4096,768]{1,0:T(8,128)(2,1)}) %all-gather.10.cloned.1.call-update) | async-done | bytes 6291472 | tf_op jit(solution)/shard_map/all_gather | solution.py:174
  107.5 4.8 convolution_convert_fusion.4
  113.3 64.7 %all-gather.8.cloned.1.call-done = bf16[12,512,512]{2,1,0:T(8,128)(2,1)} async-done(((bf16[12,512,128]{2,1,0:T(8,128)(2,1)}), bf16[12,512,512]{2,1,0:T(8,128)(2,1)}) %all-gather.8.cloned.1.call-update) | async-done | bytes 6291472 | tf_op jit(solution)/shard_map/all_gather | solution.py:165
  185.6 4.2 select_reduce_fusion
  189.7 6.8 fusion.3
  196.6 19.2 %fusion.79 = bf16[8,12,8,512]{3,2,1,0:T(8,128)(2,1)S(1)} fusion(f32[8,3,512]{2,1,0:T(4,128)S(1)} %fusion.3, f32[8,3,512]{2,1,0:T(4,128)S(1)} %select_reduce_fusion, f32[3,512,512]{1,2,0:T(8,128)S(1)} %copy-done.3, pred[8,512,512]{1,2,0:T(8,128)(4,1)S(1)} %broadcast_compare_fusion, bf16[3,96]{1,0:T(4,128)(2,1)S(1)} %fusion.99, ...), kind=kOutput, calls=%fused_computation.84 | convolution fusion | flops 1238237184 | bytes 6914624 | tf_op jit(solution)/shard_map/while/body/eval_jaxpr/sgqk,skgw->sqgw/dot_general | solution.py:100
  215.9 6.4 fusion.112
  222.9 128.7 %reduce-scatter.15.cloned.1.call-done = f32[512,768]{1,0:T(8,128)} async-done(((f32[4096,768]{1,0:T(8,128)}), f32[512,768]{1,0:T(8,128)}) %reduce-scatter.15.cloned.1.call-update) | async-done | bytes 1572880 | tf_op jit(solution)/shard_map/reduce_scatter | solution.py:181
  354.0 19.3 %collective-permute-done = bf16[512,768]{1,0:T(8,128)(2,1)S(1)} collective-permute-done((bf16[512,768]{1,0:T(8,128)(2,1)S(1)}, bf16[512,768]{1,0:T(8,128)(2,1)S(1)}, u32[]{:S(2)}, u32[]{:S(2)}) %collective-permute-start) | collective-permute-done | bytes 786464 | tf_op jit(solution)/shard_map/ppermute | solution.py:20
  373.3 30.1 %collective-permute-done.1 = bf16[512,768]{1,0:T(8,128)(2,1)S(1)} collective-permute-done((bf16[512,768]{1,0:T(8,128)(2,1)S(1)}, bf16[512,768]{1,0:T(8,128)(2,1)S(1)}, u32[]{:S(2)}, u32[]{:S(2)}) %collective-permute-start.1) | collective-permute-done | bytes 786464 | tf_op jit(solution)/shard_map/ppermute | solution.py:20
  404.3 30.0 %collective-permute-done.2 = bf16[512,768]{1,0:T(8,128)(2,1)S(1)} collective-permute-done((bf16[512,768]{1,0:T(8,128)(2,1)S(1)}, bf16[512,768]{1,0:T(8,128)(2,1)S(1)}, u32[]{:S(2)}, u32[]{:S(2)}) %collective-permute-start.2) | collective-permute-done | bytes 786464 | tf_op jit(solution)/shard_map/ppermute | solution.py:20
  435.2 13.2 %collective-permute-done.3 = bf16[512,768]{1,0:T(8,128)(2,1)S(1)} collective-permute-done((bf16[512,768]{1,0:T(8,128)(2,1)S(1)}, bf16[512,768]{1,0:T(8,128)(2,1)S(1)}, u32[]{:S(2)}, u32[]{:S(2)}) %collective-permute-start.3) | collective-permute-done | bytes 786464 | tf_op jit(solution)/shard_map/ppermute | solution.py:20
  449.3 13.2 %collective-permute-done.4 = bf16[512,768]{1,0:T(8,128)(2,1)S(1)} collective-permute-done((bf16[512,768]{1,0:T(8,128)(2,1)S(1)}, bf16[512,768]{1,0:T(8,128)(2,1)S(1)}, u32[]{:S(2)}, u32[]{:S(2)}) %collective-permute-start.4) | collective-permute-done | bytes 786464 | tf_op jit(solution)/shard_map/ppermute | solution.py:20
  463.4 13.3 %collective-permute-done.5 = bf16[512,768]{1,0:T(8,128)(2,1)} collective-permute-done((bf16[512,768]{1,0:T(8,128)(2,1)S(1)}, bf16[512,768]{1,0:T(8,128)(2,1)}, u32[]{:S(2)}, u32[]{:S(2)}) %collective-permute-start.5) | collective-permute-done | bytes 786464 | tf_op jit(solution)/shard_map/ppermute | solution.py:20
  476.7 12.0 %all_gather.49 = bf16[384,768]{0,1:T(8,128)(2,1)} all-gather(bf16[384,192]{0,1:T(8,128)(2,1)} %param.18), channel_id=1, replica_groups=mesh['gx'=4,'gy'=8] {'gx'}, dimensions={1}, use_global_device_ids=true | all-gather | bytes 737280 | tf_op jit(solution)/shard_map/all_gather | solution.py:164
  488.7 11.0 all_gather.48
  499.7 5.8 fusion.113
  511.7 8.6 fusion.31
  521.9 5.3 convolution_convert_fusion.1
  528.3 10.1 convolution_convert_fusion.2
  538.8 55.9 %reduce-scatter.19.cloned.1.call-done = bf16[512,768]{1,0:T(8,128)(2,1)} async-done(((bf16[4096,768]{1,0:T(8,128)(2,1)}), bf16[512,768]{1,0:T(8,128)(2,1)}) %reduce-scatter.19.cloned.1.call-update) | async-done | bytes 786448 | tf_op jit(solution)/shard_map/reduce_scatter | solution.py:200
  596.7 68.7 %reduce-scatter.17.cloned.1.call-done = bf16[512,768]{1,0:T(8,128)(2,1)} async-done(((bf16[4096,768]{1,0:T(8,128)(2,1)}), bf16[512,768]{1,0:T(8,128)(2,1)}) %reduce-scatter.17.cloned.1.call-update) | async-done | bytes 786448 | tf_op jit(solution)/shard_map/reduce_scatter | solution.py:190
  670.7 63.2 %all-gather.14.cloned.1.call-done = bf16[4096,768]{1,0:T(8,128)(2,1)} async-done(((bf16[512,768]{1,0:T(8,128)(2,1)}), bf16[4096,768]{1,0:T(8,128)(2,1)}) %all-gather.14.cloned.1.call-update) | async-done | bytes 6291472 | tf_op jit(solution)/shard_map/all_gather | solution.py:207
  733.9 4.8 convolution_convert_fusion.3
  739.7 16.4 %fusion = f32[8,3,512,512]{2,3,1,0:T(8,128)} fusion(f32[8,3,512]{2,1,0:T(4,128)S(1)} %log_add_fusion, f32[3,512,512]{1,2,0:T(8,128)} %copy.31, pred[8,512,512]{1,2,0:T(8,128)(4,1)S(1)} %copy-done.5, bf16[8,512,96]{1,2,0:T(8,128)(2,1)} %bitcast.66, bf16[3,96]{1,0:T(4,128)(2,1)S(1)} %fusion.99, bf16[8,512,96]{1,2,0:T(8,128)(2,1)} %bitcast.63), kind=kOutput, calls=%fused_computation | convolution fusion | flops 1229206016 | bytes 32031296 | tf_op jit(solution)/shard_map/while/body/eval_jaxpr/sub | solution.py:132
  756.1 15.4 %fusion.9 = bf16[3,512,512]{1,2,0:T(8,128)(2,1)} fusion(f32[8,3,512,512]{2,3,1,0:T(8,128)} %fusion, f32[8,3,512]{2,1,0:T(4,128)S(1)} %log_add_fusion, f32[3,512,512]{1,2,0:T(8,128)} %copy.31, pred[8,512,512]{1,2,0:T(8,128)(4,1)S(1)} %copy-done.5, bf16[3,96]{1,0:T(4,128)(2,1)S(1)} %fusion.99, bf16[8,512,96]{1,2,0:T(8,128)(2,1)} %bitcast.64, ...), kind=kOutput, calls=%fused_computation.12 | convolution fusion | flops 1240989696 | bytes 33604160 | tf_op jit(solution)/shard_map/while/body/eval_jaxpr/sqgw,skgw->sgqk/dot_general | solution.py:128
  778.7 14.6 %copy.44 = bf16[12,512,512]{1,0,2:T(8,128)(2,1)} copy(bf16[12,512,512]{2,1,0:T(8,128)(2,1)} %constant_dynamic-update-slice_fusion.16) | data formatting | bytes 12582912
  793.2 13.4 %copy.52 = bf16[64,8,12,512]{3,1,2,0:T(8,128)(2,1)} copy(bf16[64,8,12,512]{3,2,1,0:T(8,128)(2,1)} %bitcast.54) | data formatting | bytes 12582912
  806.7 8.0 fusion.71
  815.0 9.0 convolution_convert_fusion.5
  824.0 4.4 convolution_convert_fusion.7
  829.2 9.2 fusion.74
  840.0 5.4 convolution_convert_fusion.6
  845.5 4.5 convolution_convert_fusion
  850.2 25.6 %reduce-scatter.31.cloned.1.call-done = bf16[128,6144]{1,0:T(8,128)(2,1)} async-done(((bf16[512,6144]{1,0:T(8,128)(2,1)}), bf16[128,6144]{1,0:T(8,128)(2,1)}) %reduce-scatter.31.cloned.1.call-update) | async-done | bytes 1572880
  875.7 4.0 reshape.182
  879.7 4.3 copy.45
  885.3 18.2 %reduce-scatter.27.cloned.1.call-done = bf16[192,384]{1,0:T(8,128)(2,1)} async-done(((bf16[768,384]{1,0:T(8,128)(2,1)}), bf16[192,384]{1,0:T(8,128)(2,1)}) %reduce-scatter.27.cloned.1.call-update) | async-done | bytes 147472 | tf_op jit(solution)/shard_map/reduce_scatter | solution.py:239
  905.2 26.6 %reduce-scatter.29.cloned.1.call-done = bf16[384,192]{0,1:T(8,128)(2,1)} async-done(((bf16[384,768]{0,1:T(8,128)(2,1)}), bf16[384,192]{0,1:T(8,128)(2,1)}) %reduce-scatter.29.cloned.1.call-update) | async-done | bytes 147472 | tf_op jit(solution)/shard_map/reduce_scatter | solution.py:245
  933.4 25.0 %reduce-scatter.33.cloned.1.call-done = bf16[192,96]{1,0:T(8,128)(2,1)} async-done(((bf16[768,96]{1,0:T(8,128)(2,1)}), bf16[192,96]{1,0:T(8,128)(2,1)}) %reduce-scatter.33.cloned.1.call-update) | async-done | bytes 36880
  959.9 25.8 %reduce-scatter.23.cloned.1.call-done = bf16[192,96]{1,0:T(8,128)(2,1)} async-done(((bf16[768,96]{1,0:T(8,128)(2,1)}), bf16[192,96]{1,0:T(8,128)(2,1)}) %reduce-scatter.23.cloned.1.call-update) | async-done | bytes 36880 | tf_op jit(solution)/shard_map/reduce_scatter | solution.py:236
  987.1 70.5 %reduce-scatter.21.cloned.1.call-done = bf16[512,768]{1,0:T(8,128)(2,1)} async-done(((bf16[4096,768]{1,0:T(8,128)(2,1)}), bf16[512,768]{1,0:T(8,128)(2,1)}) %reduce-scatter.21.cloned.1.call-update) | async-done | bytes 786448 | tf_op jit(solution)/shard_map/reduce_scatter | solution.py:215
  1061.4 9.9 all-reduce.10
  1071.4 13.7 %all-reduce.8 = (bf16[192]{0:T(256)(128)(2,1)S(1)}, bf16[192]{0:T(256)(128)(2,1)S(1)}) all-reduce(bf16[192]{0:T(256)(128)(2,1)S(1)} %dynamic-slice.6, bf16[192]{0:T(256)(128)(2,1)S(1)} %dynamic-slice.10), channel_id=7, replica_groups=mesh['gx'=4,'gy'=8] {'gy'}, use_global_device_ids=true, to_apply=%region_16.17.clone | all-reduce | flops 384 | bytes 1536
  (181 shorter events, 74.2 us)
Async XLA Ops:
  7.2 57.5 %copy-start.27 = (s32[8,512]{1,0:T(8,128)S(1)}, s32[8,512]{1,0:T(8,128)}, u32[]{:S(2)}) copy-start(s32[8,512]{1,0:T(8,128)} %param.11) | copy-start | bytes 49156
  7.2 39.2 %all-gather.6.cloned.1.call-start = ((), (), s32[]{:S(2)}) async-start(), calls=%async_computation.10 | async-start | bytes 1769472 | tf_op jit(solution)/shard_map/all_gather | solution.py:156
  7.9 99.6 %all-gather.10.cloned.1.call-start = ((), (), s32[]{:S(2)}) async-start(), calls=%async_computation.12 | async-start | bytes 7077888 | tf_op jit(solution)/shard_map/all_gather | solution.py:174
  41.1 25.1 %copy-start.23 = (f32[768]{0:T(1024)}, f32[768]{0:T(1024)S(1)}, u32[]{:S(2)}) copy-start(f32[768]{0:T(1024)S(1)} %convert_element_type.135) | copy-start | bytes 9220
  42.4 23.8 %copy-start.25 = (f32[512]{0:T(512)}, f32[512]{0:T(512)S(1)}, u32[]{:S(2)}) copy-start(f32[512]{0:T(512)S(1)} %broadcast_multiply_fusion.1) | copy-start | bytes 6148
  43.9 22.3 %copy-start.31 = (f32[512]{0:T(512)}, f32[512]{0:T(512)S(1)}, u32[]{:S(2)}) copy-start(f32[512]{0:T(512)S(1)} %fusion.61) | copy-start | bytes 6148
  43.9 22.3 %copy-start.29 = (f32[512]{0:T(512)}, f32[512]{0:T(512)S(1)}, u32[]{:S(2)}) copy-start(f32[512]{0:T(512)S(1)} %fusion.100) | copy-start | bytes 6148
  46.3 131.8 %all-gather.8.cloned.1.call-start = ((), (), s32[]{:S(2)}) async-start(), calls=%async_computation.11 | async-start | bytes 7864320 | tf_op jit(solution)/shard_map/all_gather | solution.py:165
  47.0 304.7 %reduce-scatter.15.cloned.1.call-start = ((), (), s32[]{:S(2)}) async-start(), calls=%async_computation.13 | async-start | bytes 14155776 | tf_op jit(solution)/shard_map/reduce_scatter | solution.py:181
  56.4 56.0 %copy-start.18 = (bf16[768,96]{1,0:T(8,128)(2,1)}, bf16[768,96]{1,0:T(8,128)(2,1)S(1)}, u32[]{:S(2)}) copy-start(bf16[768,96]{1,0:T(8,128)(2,1)S(1)} %all_gather.44) | copy-start | bytes 442372
  66.2 130.3 %copy-start.4 = (pred[8,512,512]{1,2,0:T(8,128)(4,1)}, pred[8,512,512]{1,2,0:T(8,128)(4,1)S(1)}, u32[]{:S(2)}) copy-start(pred[8,512,512]{1,2,0:T(8,128)(4,1)S(1)} %broadcast_compare_fusion) | copy-start | bytes 6291460
  189.7 6.8 copy-start.3
  189.7 6.8 copy-start.20
  215.9 6.4 copy-start.6
  222.3 129.4 %copy-start = (bf16[512,768]{1,0:T(8,128)(2,1)S(1)}, bf16[512,768]{1,0:T(8,128)(2,1)}, u32[]{:S(2)}) copy-start(bf16[512,768]{1,0:T(8,128)(2,1)} %param.10) | copy-start | bytes 2359300
  222.3 277.4 %all-gather.12.cloned.1.call-start = ((), (), s32[]{:S(2)}) async-start(), calls=%async_computation.15 | async-start | bytes 7077888 | tf_op jit(solution)/shard_map/all_gather | solution.py:194
  222.9 371.9 %reduce-scatter.19.cloned.1.call-start = ((), (), s32[]{:S(2)}) async-start(), calls=%async_computation.16 | async-start | bytes 7077888 | tf_op jit(solution)/shard_map/reduce_scatter | solution.py:200
  353.9 19.4 %collective-permute-start = (bf16[512,768]{1,0:T(8,128)(2,1)S(1)}, bf16[512,768]{1,0:T(8,128)(2,1)S(1)}, u32[]{:S(2)}, u32[]{:S(2)}) collective-permute-start(bf16[512,768]{1,0:T(8,128)(2,1)S(1)} %multiply_convert_fusion.1), channel_id=1, source_target_pairs={{0,1},{1,2},{2,3},{3,4},{4,5},{5,6},{6,7},{7,0},{8,9},{9,10},{10,1... | collective-permute-start | bytes 2359304 | tf_op jit(solution)/shard_map/ppermute | solution.py:20
  373.3 30.1 %collective-permute-start.1 = (bf16[512,768]{1,0:T(8,128)(2,1)S(1)}, bf16[512,768]{1,0:T(8,128)(2,1)S(1)}, u32[]{:S(2)}, u32[]{:S(2)}) collective-permute-start(bf16[512,768]{1,0:T(8,128)(2,1)S(1)} %collective-permute-done), channel_id=1, source_target_pairs={{0,1},{1,2},{2,3},{3,4},{4,5},{5,6},{6,7},{7,0},{8,9},{9,10},{10,1... | collective-permute-start | bytes 2359304 | tf_op jit(solution)/shard_map/ppermute | solution.py:20
  404.3 30.0 %collective-permute-start.2 = (bf16[512,768]{1,0:T(8,128)(2,1)S(1)}, bf16[512,768]{1,0:T(8,128)(2,1)S(1)}, u32[]{:S(2)}, u32[]{:S(2)}) collective-permute-start(bf16[512,768]{1,0:T(8,128)(2,1)S(1)} %collective-permute-done.1), channel_id=1, source_target_pairs={{0,1},{1,2},{2,3},{3,4},{4,5},{5,6},{6,7},{7,0},{8,9},{9,10},{10,1... | collective-permute-start | bytes 2359304 | tf_op jit(solution)/shard_map/ppermute | solution.py:20
  435.2 13.2 %collective-permute-start.3 = (bf16[512,768]{1,0:T(8,128)(2,1)S(1)}, bf16[512,768]{1,0:T(8,128)(2,1)S(1)}, u32[]{:S(2)}, u32[]{:S(2)}) collective-permute-start(bf16[512,768]{1,0:T(8,128)(2,1)S(1)} %collective-permute-done.2), channel_id=1, source_target_pairs={{0,1},{1,2},{2,3},{3,4},{4,5},{5,6},{6,7},{7,0},{8,9},{9,10},{10,1... | collective-permute-start | bytes 2359304 | tf_op jit(solution)/shard_map/ppermute | solution.py:20
  449.3 13.2 %collective-permute-start.4 = (bf16[512,768]{1,0:T(8,128)(2,1)S(1)}, bf16[512,768]{1,0:T(8,128)(2,1)S(1)}, u32[]{:S(2)}, u32[]{:S(2)}) collective-permute-start(bf16[512,768]{1,0:T(8,128)(2,1)S(1)} %collective-permute-done.3), channel_id=1, source_target_pairs={{0,1},{1,2},{2,3},{3,4},{4,5},{5,6},{6,7},{7,0},{8,9},{9,10},{10,1... | collective-permute-start | bytes 2359304 | tf_op jit(solution)/shard_map/ppermute | solution.py:20
  463.4 13.3 %collective-permute-start.5 = (bf16[512,768]{1,0:T(8,128)(2,1)S(1)}, bf16[512,768]{1,0:T(8,128)(2,1)}, u32[]{:S(2)}, u32[]{:S(2)}) collective-permute-start(bf16[512,768]{1,0:T(8,128)(2,1)S(1)} %collective-permute-done.4), channel_id=1, source_target_pairs={{0,1},{1,2},{2,3},{3,4},{4,5},{5,6},{6,7},{7,0},{8,9},{9,10},{10,1... | collective-permute-start | bytes 2359304 | tf_op jit(solution)/shard_map/ppermute | solution.py:20
  476.7 28.8 %collective-permute-start.6 = (bf16[512,768]{1,0:T(8,128)(2,1)}, bf16[512,768]{1,0:T(8,128)(2,1)}, u32[]{:S(2)}, u32[]{:S(2)}) collective-permute-start(bf16[512,768]{1,0:T(8,128)(2,1)} %collective-permute-done.5), channel_id=1, source_target_pairs={{0,1},{1,2},{2,3},{3,4},{4,5},{5,6},{6,7},{7,0},{8,9},{9,10},{10,1... | collective-permute-start | bytes 2359304 | tf_op jit(solution)/shard_map/ppermute | solution.py:20
  499.7 8.3 copy-start.17
  499.7 8.4 copy-start.15
  505.5 2.7 copy-start.13
  505.5 2.7 copy-start.11
  511.6 8.6 copy-start.28
  527.3 138.0 %reduce-scatter.17.cloned.1.call-start = ((), (), s32[]{:S(2)}) async-start(), calls=%async_computation.14 | async-start | bytes 7077888 | tf_op jit(solution)/shard_map/reduce_scatter | solution.py:190
  538.4 131.0 %copy-start.7 = (bf16[512,768]{1,0:T(8,128)(2,1)S(1)}, bf16[512,768]{1,0:T(8,128)(2,1)}, u32[]{:S(2)}) copy-start(bf16[512,768]{1,0:T(8,128)(2,1)} %param.19) | copy-start | bytes 2359300
  538.4 195.5 %all-gather.14.cloned.1.call-start = ((), (), s32[]{:S(2)}) async-start(), calls=%async_computation.17 | async-start | bytes 7077888 | tf_op jit(solution)/shard_map/all_gather | solution.py:207
  670.6 205.1 %reduce-scatter.31.cloned.1.call-start = ((), (), s32[]{:S(2)}) async-start(), calls=%async_computation.23 | async-start | bytes 7864320
  670.7 69.0 %copy-start.5 = (pred[8,512,512]{1,2,0:T(8,128)(4,1)S(1)}, pred[8,512,512]{1,2,0:T(8,128)(4,1)}, u32[]{:S(2)}) copy-start(pred[8,512,512]{1,2,0:T(8,128)(4,1)} %copy-done.4) | copy-start | bytes 6291460
  774.1 3.2 copy-start.9
  806.7 96.9 %reduce-scatter.27.cloned.1.call-start = ((), (), s32[]{:S(2)}) async-start(), calls=%async_computation.21 | async-start | bytes 737280 | tf_op jit(solution)/shard_map/reduce_scatter | solution.py:239
  814.7 117.0 %reduce-scatter.29.cloned.1.call-start = ((), (), s32[]{:S(2)}) async-start(), calls=%async_computation.22 | async-start | bytes 737280 | tf_op jit(solution)/shard_map/reduce_scatter | solution.py:245
  824.0 134.4 %reduce-scatter.33.cloned.1.call-start = ((), (), s32[]{:S(2)}) async-start(), calls=%async_computation.24 | async-start | bytes 245760
  838.4 7.1 copy-start.19
  839.7 146.0 %reduce-scatter.23.cloned.1.call-start = ((), (), s32[]{:S(2)}) async-start(), calls=%async_computation.19 | async-start | bytes 245760 | tf_op jit(solution)/shard_map/reduce_scatter | solution.py:236
  845.5 212.2 %reduce-scatter.21.cloned.1.call-start = ((), (), s32[]{:S(2)}) async-start(), calls=%async_computation.18 | async-start | bytes 7077888 | tf_op jit(solution)/shard_map/reduce_scatter | solution.py:215
  850.0 207.7 %copy-start.24 = (f32[768]{0:T(1024)S(1)}, f32[768]{0:T(1024)}, u32[]{:S(2)}) copy-start(f32[768]{0:T(1024)} %copy-done.23) | copy-start | bytes 9220
  850.0 207.7 %copy-start.26 = (f32[512]{0:T(512)S(1)}, f32[512]{0:T(512)}, u32[]{:S(2)}) copy-start(f32[512]{0:T(512)} %copy-done.25) | copy-start | bytes 6148
  850.1 209.2 %copy-start.32 = (f32[512]{0:T(512)S(1)}, f32[512]{0:T(512)}, u32[]{:S(2)}) copy-start(f32[512]{0:T(512)} %copy-done.31) | copy-start | bytes 6148
  850.1 209.3 %copy-start.30 = (f32[512]{0:T(512)S(1)}, f32[512]{0:T(512)}, u32[]{:S(2)}) copy-start(f32[512]{0:T(512)} %copy-done.29) | copy-start | bytes 6148
  850.1 236.2 %copy-start.2 = (f32[512,768]{1,0:T(8,128)S(1)}, f32[512,768]{1,0:T(8,128)}, u32[]{:S(2)}) copy-start(f32[512,768]{1,0:T(8,128)} %copy-done.1) | copy-start | bytes 4718596
  850.1 236.2 %copy-start.8 = (bf16[512,768]{1,0:T(8,128)(2,1)S(1)}, bf16[512,768]{1,0:T(8,128)(2,1)}, u32[]{:S(2)}) copy-start(bf16[512,768]{1,0:T(8,128)(2,1)} %param.19) | copy-start | bytes 2359300
  850.1 242.4 %reduce-scatter.25.cloned.1.call-start = ((), (), s32[]{:S(2)}) async-start(), calls=%async_computation.20 | async-start | bytes 1769472 | tf_op jit(solution)/shard_map/reduce_scatter | solution.py:259
  (8 other events, 9.2 us)
Sparse Core Ops, SparseCore 0:
  9.6 27.8 all-gather.5
  46.4 61.0 all-gather.9
  109.4 68.6 all-gather.7
  222.4 129.2 reduce-scatter.14
  353.2 83.2 all-gather.11
  527.4 67.3 reduce-scatter.18
  597.1 68.1 reduce-scatter.16
  670.7 63.1 all-gather.13
  806.8 68.8 reduce-scatter.30
  878.4 25.0 reduce-scatter.26
  906.6 25.0 reduce-scatter.28
  934.4 23.9 reduce-scatter.32
  961.7 23.9 reduce-scatter.22
  987.9 69.7 reduce-scatter.20
  1059.8 32.6 reduce-scatter.24
